TPU v7x, 512 devices: a whole 4x4x16 slice. The times are simulated.
512 devices in a mesh: dp: 4 (over x), cand: 32 (over z, core), tensor: 4 (over y).
Axes of the slice: x: 4, y: 4, z: 16, core: 2. Of those that a mesh axis runs over, the one named last changes fastest.
Arguments:
- context: bfloat16 [8, 4096, 3584], P('dp', 'cand', 'tensor'), may hold values from -12 to 12
- residual: bfloat16 [8, 4096, 3584], P('dp', ('cand', 'tensor')), may hold values from -36 to 36
- out_weight: bfloat16 [3584, 3584], P('cand', 'tensor'), may hold values from -0.09375 to 0.09375
- adapter_down: bfloat16 [3584, 16], P('tensor'), may hold values from -0.09375 to 0.09375
- adapter_up_weight: bfloat16 [16, 3584], replicated, may hold values from -1.5 to 1.5
- norm_gain: float32 [3584], replicated, may hold values from 0.5 to 1.5
- score_weight: float32 [3584], replicated, may hold values from -0.09375 to 0.09375
- teacher: bfloat16 [8, 4096, 4096], P('dp', 'cand', 'tensor'), may hold values from 0.019897461 to 0.9765625
- pair_mask: int32 [8, 4096, 4096], P('dp', 'cand', 'tensor'), may hold values from 0 to 1, as said below
- loss_scale: float32 [8], P('dp'), may hold values from 65536 to 262144
Outputs:
- context_grad: bfloat16 [8, 4096, 3584], P('dp', 'cand', 'tensor')
- residual_gradient: bfloat16 [8, 4096, 3584], P('dp', ('cand', 'tensor'))
- down_grad: float32 [3584, 16], P('tensor')
- up_weight_gradient: float32 [16, 3584], P(None, 'tensor')
- pair_loss: float32 [8], P('dp')
Inputs may be any that keep to these rules, and one draw needn't show every extreme that they name: pair_mask holds 0 or 1; with P = 32, every pair (i, j) whose group j // P lies 4096 / (2P) groups after i // P, counted round over the 4096 / P groups, is valid.
All inputs are finite; a program needn't handle non-finite values.
Results may differ from a plain program's by a relative error of at most 0.02.
Values may be sent and summed in bfloat16 or wider, within the bound.
No kernel may reach another device: no remote copies, remote signals or barrier semaphores. Data moves between devices by JAX's collectives and lax.ppermute only.
A program may use at most 64 MiB of HBM per device.

v0:
```python
import jax
import jax.numpy as jnp
from jax import lax
from jax.sharding import PartitionSpec as P

ADAPTER_SCALE = 0.5
epsilon = 1e-06


def rounded(term):
    return lax.optimization_barrier(term.astype(jnp.bfloat16)).astype(jnp.float32)


def pair_terms(all_scores, own_scores, teacher, valid_pairs, row_start, col_start):
    column_scores = lax.dynamic_slice_in_dim(all_scores, col_start, teacher.shape[2], 1)
    margin = own_scores[:, :, None] - column_scores[:, None, :]
    target = teacher.astype(jnp.float32)
    total = jnp.sum(valid_pairs * (jax.nn.softplus(margin) - target * margin), axis=(1, 2))
    slope = valid_pairs * (jax.nn.sigmoid(margin) - target)
    blank = jnp.zeros(all_scores.shape, jnp.float32)
    row_part = lax.dynamic_update_slice_in_dim(blank, jnp.sum(slope, axis=2), row_start, 1)
    column_part = lax.dynamic_update_slice_in_dim(blank, jnp.sum(slope, axis=1), col_start, 1)
    return (total, row_part - column_part)


def on_device(
    context,
    residual,
    out_weight,
    adapter_down,
    adapter_up_weight,
    norm_gain,
    score_weight,
    teacher,
    pair_mask,
    loss_scale,
):
    cand_rows = context.shape[1]
    tensor_count = lax.axis_size("tensor")
    share = cand_rows // tensor_count
    tensor_index = lax.axis_index("tensor")
    group_index = lax.axis_index("cand")
    valid_pairs = pair_mask.astype(jnp.float32)
    mask_count = jnp.sum(valid_pairs, axis=(1, 2))
    count = lax.psum(mask_count, ("cand", "tensor"))
    low_terms = rounded(
        jnp.einsum("qch,hr->qcr", context, adapter_down, preferred_element_type=jnp.float32)
    )
    full_weight = lax.all_gather(out_weight, "cand", axis=0, tiled=True)
    head_terms = jnp.einsum("qch,dh->qcd", context, full_weight, preferred_element_type=jnp.float32)
    head_terms = rounded(head_terms)
    summed_output, low_sum = (
        lax.psum_scatter(
            head_terms.astype(jnp.bfloat16), "tensor", scatter_dimension=1, tiled=True
        ).astype(jnp.float32),
        lax.psum_scatter(
            low_terms.astype(jnp.bfloat16), "tensor", scatter_dimension=1, tiled=True
        ).astype(jnp.float32),
    )
    adapter_input_rows = low_sum.astype(jnp.bfloat16)
    lifted_rows = jnp.einsum(
        "qcr,rd->qcd", adapter_input_rows, adapter_up_weight, preferred_element_type=jnp.float32
    )
    hidden_state = (
        residual.astype(jnp.float32) + summed_output + ADAPTER_SCALE * lifted_rows
    ).astype(jnp.bfloat16)
    hidden_wide = hidden_state.astype(jnp.float32)
    inv_rms = lax.rsqrt(jnp.mean(hidden_wide * hidden_wide, axis=2, keepdims=True) + epsilon)
    scores = jnp.sum(hidden_wide * inv_rms * norm_gain * score_weight, axis=2)
    all_scores = lax.all_gather(scores, ("cand", "tensor"), axis=1, tiled=True)
    own_start = group_index * cand_rows + tensor_index * share
    row_start = group_index * cand_rows
    col_start = tensor_index * teacher.shape[2]
    own_scores = lax.dynamic_slice_in_dim(all_scores, row_start, cand_rows, 1)
    total, score_vector = pair_terms(
        all_scores, own_scores, teacher, valid_pairs, row_start, col_start
    )
    summed_grad, loss_sum = lax.psum((score_vector, total), ("cand", "tensor"))
    pair_loss = loss_sum / count
    factor = loss_scale / count
    score_grad = lax.dynamic_slice_in_dim(summed_grad, own_start, share, 1) * factor[:, None]
    back_step = score_grad[:, :, None] * norm_gain * score_weight
    grad_hidden = inv_rms * back_step - hidden_wide * inv_rms**3 * jnp.mean(
        hidden_wide * back_step, axis=2, keepdims=True
    )
    grad_rows = grad_hidden.astype(jnp.bfloat16)
    adapter_rows = (
        ADAPTER_SCALE
        * jnp.einsum(
            "qcd,rd->qcr", grad_rows, adapter_up_weight, preferred_element_type=jnp.float32
        )
    ).astype(jnp.bfloat16)
    full_grads, full_adapter = (
        lax.all_gather(grad_rows, "tensor", axis=1, tiled=True),
        lax.all_gather(adapter_rows, "tensor", axis=1, tiled=True),
    )
    up_partial_gradient = ADAPTER_SCALE * jnp.einsum(
        "qcr,qcd->rd", adapter_input_rows, grad_rows, preferred_element_type=jnp.float32
    )
    up_share = lax.psum_scatter(
        up_partial_gradient.astype(jnp.bfloat16), "tensor", scatter_dimension=1, tiled=True
    ).astype(jnp.float32)
    adapter_back = jnp.einsum(
        "qcr,hr->qch", full_adapter, adapter_down, preferred_element_type=jnp.float32
    )
    context_wide = (
        jnp.einsum("qcd,dh->qch", full_grads, full_weight, preferred_element_type=jnp.float32)
        + adapter_back
    )
    context_grad = context_wide.astype(jnp.bfloat16)
    down_local = jnp.einsum(
        "qch,qcr->hr", context, full_adapter, preferred_element_type=jnp.float32
    )
    down_grad, up_weight_gradient = lax.psum((down_local, up_share), ("dp", "cand"))
    return (context_grad, grad_rows, down_grad, up_weight_gradient, pair_loss)


def solution(mesh):
    in_specs = (
        P("dp", "cand", "tensor"),
        P("dp", ("cand", "tensor"), None),
        P("cand", "tensor"),
        P("tensor", None),
        P(),
        P(),
        P(),
        P("dp", "cand", "tensor"),
        P("dp", "cand", "tensor"),
        P("dp"),
    )
    out_specs = (
        P("dp", "cand", "tensor"),
        P("dp", ("cand", "tensor"), None),
        P("tensor", None),
        P(None, "tensor"),
        P("dp"),
    )
    return jax.shard_map(
        on_device, mesh=mesh, in_specs=in_specs, out_specs=out_specs, check_vma=False
    )
```

profile of v0, /device:TPU:16, one launch (start us, length us, event | category | flops | bytes accessed | tf_op | source)
XLA Modules:
  0.0 1309.3 jit_solution(4041656282521602248)
XLA Ops:
  8.0 0.0 copy-start
  8.0 0.0 all-gather.4.cloned.1.call-start
  8.1 0.7 all-gather.4.cloned.1.call-update
  8.7 0.0 reduce-scatter.10.cloned.1.call-start
  8.8 0.2 copy-done
  9.0 0.9 convolution_convert_fusion
  10.0 0.2 copy.20
  10.2 0.7 reshape.41
  10.9 0.0 reduce-scatter.10.cloned.1.call-update
  10.9 0.0 copy-start.4
  10.9 0.0 copy-start.7
  10.9 0.0 copy-start.2
  11.0 0.0 reduce-scatter.8.cloned.1.call-start
  11.0 81.7 %all-gather.4.cloned.1.call-done = bf16[3584,896]{1,0:T(8,128)(2,1)} async-done(((bf16[112,896]{1,0:T(8,128)(2,1)}), bf16[3584,896]{1,0:T(8,128)(2,1)}) %all-gather.4.cloned.1.call-update) | async-done | bytes 6422544 | tf_op jit(solution)/shard_map/all_gather | solution.py:49
  92.7 6.2 fusion.4
  98.9 0.0 reduce-scatter.8.cloned.1.call-update
  98.9 0.0 reduce-scatter.12.cloned.1.call-start
  98.9 0.0 reduce-scatter.10.cloned.1.call-done
  99.0 0.8 reshape.42
  99.8 0.7 copy.21
  100.4 29.0 %reduce-scatter.8.cloned.1.call-done = bf16[2,32,3584]{2,1,0:T(8,128)(2,1)} async-done(((bf16[2,128,3584]{2,1,0:T(8,128)(2,1)}), bf16[2,32,3584]{2,1,0:T(8,128)(2,1)}) %reduce-scatter.8.cloned.1.call-update) | async-done | bytes 458768 | tf_op jit(solution)/shard_map/reduce_scatter | solution.py:53
  129.5 1.5 multiply_reduce_fusion.2
  131.0 0.3 multiply_reduce_fusion.1
  131.3 140.3 %all-gather = f32[128,32,2]{1,2,0:T(2,128)S(1)} all-gather(f32[1,32,2]{1,2,0:T(2,128)S(1)} %bitcast.57), channel_id=1, replica_groups=mesh['dp'=4,'cand'=32,'tensor'=4] {'cand','tensor'}, dimensions={0}, use_global_device_ids=true | all-gather | bytes 33024 | tf_op jit(solution)/shard_map/all_gather | solution.py:70
  271.6 0.1 reshape.35
  271.8 1.2 fusion.24
  273.0 0.2 fusion.31
  273.3 493.2 %all-reduce = (f32[2,4096]{1,0:T(2,128)S(1)}, f32[2]{0:T(128)S(1)}, f32[2]{0:T(128)S(1)}) all-reduce(f32[2,4096]{1,0:T(2,128)S(1)} %sub.29, f32[2]{0:T(128)S(1)} %get-tuple-element.6, f32[2]{0:T(128)S(1)} %get-tuple-element.5), channel_id=1, replica_groups=mesh['dp'=4,'cand'=32,'tensor'=4] {'cand','tensor'}, use_global_device_ids=true, to_apply=%region_6.7 | all-reduce | flops 8196 | bytes 65568 | tf_op jit(solution)/shard_map/psum | solution.py:78
  766.4 1.2 fusion.32
  767.6 0.1 fusion.30
  767.7 0.3 multiply_reduce_fusion
  768.0 0.3 subtract_convert_fusion
  768.3 0.0 copy-start.1
  768.3 0.2 fusion.11
  768.5 1.3 copy.22
  769.8 0.0 reduce-scatter.12.cloned.1.call-update
  769.9 0.0 all-gather.6.cloned.1.call-start
  769.9 0.7 all-gather.6.cloned.1.call-update
  770.6 1.4 fusion.13
  772.0 0.1 copy.17
  772.1 13.7 %all_gather.15 = bf16[2,128,16]{2,0,1:T(2,128)(2,1)S(1)} all-gather(bf16[2,32,16]{2,0,1:T(2,128)(2,1)S(1)} %copy.17), channel_id=1, replica_groups=mesh['dp'=4,'cand'=32,'tensor'=4] {'tensor'}, dimensions={1}, use_global_device_ids=true | all-gather | bytes 10240 | tf_op jit(solution)/shard_map/all_gather | solution.py:95
  785.8 0.1 copy.18
  785.9 0.2 convolution_bitcast_fusion.1
  786.1 13.0 reduce-scatter.12.cloned.1.call-done
  799.1 1.0 copy.23
  800.1 495.1 %all-reduce.3 = (f32[896,16]{0,1:T(8,128)}, f32[16,896]{1,0:T(8,128)}) all-reduce(f32[896,16]{0,1:T(8,128)S(1)} %convolution_bitcast_fusion.1, bf16[16,896]{1,0:T(8,128)(2,1)S(1)} %copy.23), channel_id=1, replica_groups=mesh['dp'=4,'cand'=32,'tensor'=4] {'dp','cand'}, use_global_device_ids=true, to_apply=%region_10.11 | all-reduce | flops 28672 | bytes 200704 | tf_op jit(solution)/shard_map/psum | solution.py:114
  1295.2 5.5 fusion
  1300.6 1.1 fusion.12
  (25 shorter events, 0.2 us)
Async XLA Ops:
  8.0 1.0 copy-start
  8.0 84.7 %all-gather.4.cloned.1.call-start = ((), (), s32[]{:S(2)}) async-start(), calls=%async_computation.3 | async-start | bytes 6623232 | tf_op jit(solution)/shard_map/all_gather | solution.py:49
  8.7 90.2 %reduce-scatter.10.cloned.1.call-start = ((), (), s32[]{:S(2)}) async-start(), calls=%async_computation.6 | async-start | bytes 40960
  10.9 118.6 %copy-start.4 = (bf16[2,32,3584]{2,1,0:T(8,128)(2,1)S(1)}, bf16[2,32,3584]{2,1,0:T(8,128)(2,1)}, u32[]{:S(2)}) copy-start(bf16[2,32,3584]{2,1,0:T(8,128)(2,1)} %param.11) | copy-start | bytes 1376260
  10.9 118.6 %copy-start.5 = (bf16[16,3584]{1,0:T(8,128)(2,1)S(1)}, bf16[16,3584]{1,0:T(8,128)(2,1)}, u32[]{:S(2)}) copy-start(bf16[16,3584]{1,0:T(8,128)(2,1)} %param.14) | copy-start | bytes 344068
  10.9 120.1 %copy-start.6 = (f32[3584]{0:T(1024)S(1)}, f32[3584]{0:T(1024)}, u32[]{:S(2)}) copy-start(f32[3584]{0:T(1024)} %param.16) | copy-start | bytes 43012
  10.9 120.1 %copy-start.7 = (f32[3584]{0:T(1024)S(1)}, f32[3584]{0:T(1024)}, u32[]{:S(2)}) copy-start(f32[3584]{0:T(1024)} %param.15) | copy-start | bytes 43012
  10.9 260.8 %copy-start.2 = (s32[2,128,1024]{2,1,0:T(8,128)S(1)}, s32[2,128,1024]{2,1,0:T(8,128)}, u32[]{:S(2)}) copy-start(s32[2,128,1024]{2,1,0:T(8,128)} %param.18) | copy-start | bytes 3145732
  11.0 260.8 %copy-start.3 = (bf16[2,128,1024]{2,1,0:T(8,128)(2,1)S(1)}, bf16[2,128,1024]{2,1,0:T(8,128)(2,1)}, u32[]{:S(2)}) copy-start(bf16[2,128,1024]{2,1,0:T(8,128)(2,1)} %param.17) | copy-start | bytes 1572868
  11.0 118.5 %reduce-scatter.8.cloned.1.call-start = ((), (), s32[]{:S(2)}) async-start(), calls=%async_computation.4 | async-start | bytes 2293760 | tf_op jit(solution)/shard_map/reduce_scatter | solution.py:53
  98.9 700.2 %reduce-scatter.12.cloned.1.call-start = ((), (), s32[]{:S(2)}) async-start(), calls=%async_computation.7 | async-start | bytes 1146880
  130.9 637.3 %copy-start.9 = (bf16[2,32,16]{1,2,0:T(8,128)(2,1)S(1)}, bf16[2,32,16]{1,2,0:T(8,128)(2,1)}, u32[]{:S(2)}) copy-start(bf16[2,32,16]{1,2,0:T(8,128)(2,1)} %copy.21) | copy-start | bytes 6148
  768.3 1.7 copy-start.1
  769.9 525.3 %all-gather.6.cloned.1.call-start = ((), (), s32[]{:S(2)}) async-start(), calls=%async_computation.5 | async-start | bytes 2293760 | tf_op jit(solution)/shard_map/all_gather | solution.py:94
  1295.2 5.5 copy-start.8
Sparse Core Ops, SparseCore 0:
  11.2 81.4 all-gather.3
Sparse Core Ops, SparseCore 1:
  12.6 30.7 reduce-scatter.9
  99.0 30.5 reduce-scatter.7
  769.9 29.1 reduce-scatter.11
  802.0 36.1 all-gather.5
where the time goes:
time: 1310 us
  blocking collectives  1140 us (87%)
  waiting for transfers between devices  125 us (10%)
  matrix products  16.9 us (1%)
  between operations  15.9 us (1%)
    psum x1, blocking collectives, on_device(): lax.psum((down_local, up_share), ('dp', 'cand'))  495 us
    psum x1, blocking collectives, on_device(): summed_grad, loss_sum = lax.psum((score_vector, total), ('cand', 'tensor'))  493 us
    all_gather x1, blocking collectives, on_device(): all_scores = lax.all_gather(scores, ('cand', 'tensor'), axis=1, tiled=True)  140 us
    all_gather x1, waiting for transfers between devices, on_device(): full_weight = lax.all_gather(out_weight, 'cand', axis=0, tiled=True)  81.7 us
    reduce_scatter x1, waiting for transfers between devices, on_device(): lax.psum_scatter(head_terms.astype(jnp.bfloat16), 'tensor', scatter_dimen...  29 us
  transfers between devices with their start and end apart: 5, of which 3 were waited for; matrix products, arithmetic and copies ran while one was open for 1% of the time, Pallas kernels for 0%

commit v1 on v0

--- a/solution.py
+++ b/solution.py
@@ -67,7 +67,12 @@
     hidden_wide = hidden_state.astype(jnp.float32)
     inv_rms = lax.rsqrt(jnp.mean(hidden_wide * hidden_wide, axis=2, keepdims=True) + epsilon)
     scores = jnp.sum(hidden_wide * inv_rms * norm_gain * score_weight, axis=2)
-    all_scores = lax.all_gather(scores, ("cand", "tensor"), axis=1, tiled=True)
+    all_scores = jnp.concatenate(
+        lax.all_to_all(
+            jnp.stack([scores] * lax.axis_size(("cand", "tensor"))), ("cand", "tensor"), 0, 0
+        ),
+        axis=1,
+    )
     own_start = group_index * cand_rows + tensor_index * share
     row_start = group_index * cand_rows
     col_start = tensor_index * teacher.shape[2]

time: 1310 us -> 1190 us (0.908)
  blocking collectives: 1140 us -> 998 us
  starting transfers between devices: 0.21 us -> 16.7 us
    all_gather x1 -> x0, blocking collectives: 140 us -> none  [on_device(): all_scores = lax.all_gather(scores, ('cand', 'tensor'), axis=1, tiled=True)]
    all_to_all x0 -> x1, starting transfers between devices: none -> 16.5 us  [on_device(): lax.all_to_all(jnp.stack([scores] * lax.axis_size(('cand', 'tensor'))), (...]
    all_to_all x0 -> x1, waiting for transfers between devices: none -> 15.9 us  [on_device(): lax.all_to_all(jnp.stack([scores] * lax.axis_size(('cand', 'tensor'))), (...]
  transfers between devices with their start and end apart: 5 -> 6, of which waited for: 3 -> 4; matrix products, arithmetic and copies ran while one was open for 1% -> 1% of each run, Pallas kernels for 0% -> 0%
where the time goes in v1:
time: 1190 us
  blocking collectives  998 us (84%)
  waiting for transfers between devices  137 us (12%)
  matrix products  16.9 us (1%)
  starting transfers between devices  16.7 us (1%)
  between operations  15.9 us (1%)
    psum x1, blocking collectives, on_device(): lax.psum((down_local, up_share), ('dp', 'cand'))  495 us
    psum x1, blocking collectives, on_device(): summed_grad, loss_sum = lax.psum((score_vector, total), ('cand', 'tensor'))  489 us
    all_gather x1, waiting for transfers between devices, on_device(): full_weight = lax.all_gather(out_weight, 'cand', axis=0, tiled=True)  81.7 us
    reduce_scatter x1, waiting for transfers between devices, on_device(): lax.psum_scatter(head_terms.astype(jnp.bfloat16), 'tensor', scatter_dimen...  29.1 us
  transfers between devices with their start and end apart: 6, of which 4 were waited for; matrix products, arithmetic and copies ran while one was open for 1% of the time, Pallas kernels for 0%

profile of v1, /device:TPU:16, one launch (start us, length us, event | category | flops | bytes accessed | tf_op | source)
XLA Modules:
  0.0 1194.3 jit_solution(7880603552292676590)
XLA Ops:
  8.0 0.0 copy-start
  8.0 0.0 all-gather.3.cloned.1.call-start
  8.1 0.7 all-gather.3.cloned.1.call-update
  8.7 0.0 reduce-scatter.10.cloned.1.call-start
  8.8 0.2 copy-done
  9.0 0.9 convolution_convert_fusion
  10.0 0.2 copy.19
  10.2 0.7 reshape.49
  10.9 0.0 reduce-scatter.10.cloned.1.call-update
  10.9 0.0 copy-start.4
  11.0 0.0 reduce-scatter.8.cloned.1.call-start
  11.0 81.7 %all-gather.3.cloned.1.call-done = bf16[3584,896]{1,0:T(8,128)(2,1)} async-done(((bf16[112,896]{1,0:T(8,128)(2,1)}), bf16[3584,896]{1,0:T(8,128)(2,1)}) %all-gather.3.cloned.1.call-update) | async-done | bytes 6422544 | tf_op jit(solution)/shard_map/all_gather | solution.py:49
  92.7 6.2 fusion.4
  98.9 0.0 reduce-scatter.8.cloned.1.call-update
  98.9 0.0 reduce-scatter.10.cloned.1.call-done
  98.9 0.8 reshape.50
  99.7 0.7 copy.20
  100.4 29.1 %reduce-scatter.8.cloned.1.call-done = bf16[2,32,3584]{2,1,0:T(8,128)(2,1)} async-done(((bf16[2,128,3584]{2,1,0:T(8,128)(2,1)}), bf16[2,32,3584]{2,1,0:T(8,128)(2,1)}) %reduce-scatter.8.cloned.1.call-update) | async-done | bytes 458768 | tf_op jit(solution)/shard_map/reduce_scatter | solution.py:53
  129.5 1.4 multiply_reduce_fusion.2
  131.0 0.3 multiply_reduce_fusion.1
  131.3 0.7 stack.2
  132.0 16.5 %all-to-all-start = ((f32[128,2,32]{2,1,0:T(2,128)}), f32[128,2,32]{2,1,0:T(2,128)S(1)}, u32[]{:S(2)}, u32[]{:S(2)}) async-start(f32[128,2,32]{2,1,0:T(2,128)} %stack.2), calls=%async_computation.1 | async-start | bytes 262144 | tf_op jit(solution)/shard_map/all_to_all | solution.py:71
  148.5 0.0 reduce-scatter.12.cloned.1.call-start
  148.5 15.9 %all-to-all-done = f32[128,2,32]{2,1,0:T(2,128)S(1)} async-done(((f32[128,2,32]{2,1,0:T(2,128)}), f32[128,2,32]{2,1,0:T(2,128)S(1)}, u32[]{:S(2)}, u32[]{:S(2)}) %all-to-all-start) | async-done | bytes 32800 | tf_op jit(solution)/shard_map/all_to_all | solution.py:71
  164.5 0.1 reshape.43
  164.7 1.2 fusion.24
  165.9 0.2 fusion.30
  166.2 489.2 %all-reduce = (f32[2,4096]{1,0:T(2,128)S(1)}, f32[2]{0:T(128)S(1)}, f32[2]{0:T(128)S(1)}) all-reduce(f32[2,4096]{1,0:T(2,128)S(1)} %sub.29, f32[2]{0:T(128)S(1)} %get-tuple-element.6, f32[2]{0:T(128)S(1)} %get-tuple-element.5), channel_id=1, replica_groups=mesh['dp'=4,'cand'=32,'tensor'=4] {'cand','tensor'}, use_global_device_ids=true, to_apply=%region_6.7 | all-reduce | flops 8196 | bytes 65568 | tf_op jit(solution)/shard_map/psum | solution.py:83
  655.4 1.2 fusion.31
  656.5 0.1 fusion.29
  656.6 0.3 multiply_reduce_fusion
  656.9 0.3 subtract_convert_fusion
  657.2 0.0 copy-start.1
  657.2 0.2 fusion.11
  657.5 1.3 copy.21
  658.8 0.0 reduce-scatter.12.cloned.1.call-update
  658.8 0.0 all-gather.5.cloned.1.call-start
  658.8 0.7 all-gather.5.cloned.1.call-update
  659.5 1.4 fusion.13
  660.9 0.1 copy.16
  661.1 13.8 %all_gather.11 = bf16[2,128,16]{2,0,1:T(2,128)(2,1)S(1)} all-gather(bf16[2,32,16]{2,0,1:T(2,128)(2,1)S(1)} %copy.16), channel_id=1, replica_groups=mesh['dp'=4,'cand'=32,'tensor'=4] {'tensor'}, dimensions={1}, use_global_device_ids=true | all-gather | bytes 10240 | tf_op jit(solution)/shard_map/all_gather | solution.py:100
  674.9 0.1 copy.17
  674.9 0.2 convolution_bitcast_fusion.1
  675.1 8.9 reduce-scatter.12.cloned.1.call-done
  684.1 1.0 copy.22
  685.1 495.0 %all-reduce.3 = (f32[896,16]{0,1:T(8,128)}, f32[16,896]{1,0:T(8,128)}) all-reduce(f32[896,16]{0,1:T(8,128)S(1)} %convolution_bitcast_fusion.1, bf16[16,896]{1,0:T(8,128)(2,1)S(1)} %copy.22), channel_id=1, replica_groups=mesh['dp'=4,'cand'=32,'tensor'=4] {'dp','cand'}, use_global_device_ids=true, to_apply=%region_10.11 | all-reduce | flops 28672 | bytes 200704 | tf_op jit(solution)/shard_map/psum | solution.py:119
  1180.1 5.5 fusion
  1185.6 1.1 fusion.12
  (27 shorter events, 0.2 us)
Async XLA Ops:
  8.0 1.0 copy-start
  8.0 84.7 %all-gather.3.cloned.1.call-start = ((), (), s32[]{:S(2)}) async-start(), calls=%async_computation.4 | async-start | bytes 6623232 | tf_op jit(solution)/shard_map/all_gather | solution.py:49
  8.7 90.2 %reduce-scatter.10.cloned.1.call-start = ((), (), s32[]{:S(2)}) async-start(), calls=%async_computation.7 | async-start | bytes 40960
  10.9 118.6 %copy-start.4 = (bf16[2,32,3584]{2,1,0:T(8,128)(2,1)S(1)}, bf16[2,32,3584]{2,1,0:T(8,128)(2,1)}, u32[]{:S(2)}) copy-start(bf16[2,32,3584]{2,1,0:T(8,128)(2,1)} %param.11) | copy-start | bytes 1376260
  10.9 118.6 %copy-start.5 = (bf16[16,3584]{1,0:T(8,128)(2,1)S(1)}, bf16[16,3584]{1,0:T(8,128)(2,1)}, u32[]{:S(2)}) copy-start(bf16[16,3584]{1,0:T(8,128)(2,1)} %param.14) | copy-start | bytes 344068
  10.9 120.1 %copy-start.6 = (f32[3584]{0:T(1024)S(1)}, f32[3584]{0:T(1024)}, u32[]{:S(2)}) copy-start(f32[3584]{0:T(1024)} %param.16) | copy-start | bytes 43012
  10.9 120.1 %copy-start.7 = (f32[3584]{0:T(1024)S(1)}, f32[3584]{0:T(1024)}, u32[]{:S(2)}) copy-start(f32[3584]{0:T(1024)} %param.15) | copy-start | bytes 43012
  10.9 153.7 %copy-start.2 = (s32[2,128,1024]{2,1,0:T(8,128)S(1)}, s32[2,128,1024]{2,1,0:T(8,128)}, u32[]{:S(2)}) copy-start(s32[2,128,1024]{2,1,0:T(8,128)} %param.18) | copy-start | bytes 3145732
  11.0 153.7 %copy-start.3 = (bf16[2,128,1024]{2,1,0:T(8,128)(2,1)S(1)}, bf16[2,128,1024]{2,1,0:T(8,128)(2,1)}, u32[]{:S(2)}) copy-start(bf16[2,128,1024]{2,1,0:T(8,128)(2,1)} %param.17) | copy-start | bytes 1572868
  11.0 118.5 %reduce-scatter.8.cloned.1.call-start = ((), (), s32[]{:S(2)}) async-start(), calls=%async_computation.5 | async-start | bytes 2293760 | tf_op jit(solution)/shard_map/reduce_scatter | solution.py:53
  131.0 526.2 %copy-start.9 = (bf16[2,32,16]{1,2,0:T(8,128)(2,1)S(1)}, bf16[2,32,16]{1,2,0:T(8,128)(2,1)}, u32[]{:S(2)}) copy-start(bf16[2,32,16]{1,2,0:T(8,128)(2,1)} %copy.20) | copy-start | bytes 6148
  132.0 32.5 %all-to-all-start = ((f32[128,2,32]{2,1,0:T(2,128)}), f32[128,2,32]{2,1,0:T(2,128)S(1)}, u32[]{:S(2)}, u32[]{:S(2)}) async-start(f32[128,2,32]{2,1,0:T(2,128)} %stack.2), calls=%async_computation.1 | async-start | bytes 262144 | tf_op jit(solution)/shard_map/all_to_all | solution.py:71
  148.5 535.6 %reduce-scatter.12.cloned.1.call-start = ((), (), s32[]{:S(2)}) async-start(), calls=%async_computation.8 | async-start | bytes 1146880
  657.2 1.7 copy-start.1
  658.8 521.3 %all-gather.5.cloned.1.call-start = ((), (), s32[]{:S(2)}) async-start(), calls=%async_computation.6 | async-start | bytes 2293760 | tf_op jit(solution)/shard_map/all_gather | solution.py:99
  1180.1 5.5 copy-start.8
Sparse Core Ops, SparseCore 0:
  11.2 81.4 all-gather.2
Sparse Core Ops, SparseCore 1:
  12.6 30.7 reduce-scatter.9
  99.0 30.5 reduce-scatter.7
  658.9 25.1 reduce-scatter.11
  687.0 36.0 all-gather.4
